TPU v7x, 32 devices: a whole 2x2x4 slice. The times are simulated.
32 devices in a mesh: crops: 2 (over y), xy: 4 (over z), gz: 2 (over x), lab: 2 (over core).
Axes of the slice: x: 2, y: 2, z: 4, core: 2. Of those that a mesh axis runs over, the one named last changes fastest.
Arguments:
- image: bfloat16 [16, 32, 64, 128], P('lab', ('crops', 'xy'), 'gz'), parts along dimension 1, may hold values from -6 to 6
- filt: bfloat16 [3, 16, 3, 3, 3], replicated, may hold values from -0.3125 to 0.3125
- planted_colours: int32 [32, 64, 128], P(('crops', 'xy'), 'gz'), parts along dimension 0, may hold values from 0 to 63
- likelihoods: float32 [8, 32, 64, 128], P('lab', ('crops', 'xy'), 'gz'), parts along dimension 1, may hold values from 0 to 1
- loss_slope: float32 [8, 32, 64, 128], P('lab', ('crops', 'xy'), 'gz'), parts along dimension 1, may hold values from -5.25 to 5.25
Outputs:
- grad_image: bfloat16 [16, 32, 64, 128], P('lab', ('crops', 'xy'), 'gz'), parts along dimension 1
- grad_filter: float32 [6, 16, 3, 3, 3], P('crops', 'lab'), parts along dimension 0
There are 2 independent parts, one for each index of `crops`. A program takes and returns all parts, laid end to end along the dimension named above; an argument that names none is the same for every part. Nothing has to cross between parts.
Inputs may be any that keep to these rules, and one draw needn't show every extreme that they name: `planted_colours`: A value below 8 marks a seed of that colour; any other value marks an unseeded cell.
All inputs are finite; a program needn't handle non-finite values.
Results may differ from a plain program's by a relative error of at most 0.015.
Values may be sent and summed in bfloat16 or wider, within the bound.
No kernel may reach another device: no remote copies, remote signals or barrier semaphores. Data moves between devices by JAX's collectives and lax.ppermute only.
A program may use at most 64 MiB of HBM per device.

v0:
```python
import jax
import jax.numpy as jnp
from jax import lax
from jax.sharding import PartitionSpec as P

ITERS = 3


def with_halo(cells, sides, width):
    for axis, dim in sides:
        count = lax.axis_size(axis)
        ends = count - 1
        head = lax.slice_in_dim(cells, 0, width, axis=dim)
        tail = lax.slice_in_dim(cells, cells.shape[dim] - width, cells.shape[dim], axis=dim)
        cells = jnp.concatenate(
            [
                lax.ppermute(tail, axis, [(i, (i + 1) % count) for i in range(ends)]),
                cells,
                lax.ppermute(head, axis, [((i + 1) % count, i) for i in range(ends)]),
            ],
            axis=dim,
        )
    return cells


def passed_along(block, axis, distance):
    devices = range(lax.axis_size(axis))
    route = [(i - distance, i) for i in devices if i - distance in devices]
    return lax.ppermute(block, axis, route)


def offsets():
    return [
        (first, second, third) for first in range(3) for second in range(3) for third in range(3)
    ]


def correlate(weights, wide, rows_x, rows_z, rows_y):
    grand_quantity = jnp.zeros((weights.shape[0], rows_x, rows_z, rows_y), jnp.float32)
    for first, second, third in offsets():
        window = wide[:, first : first + rows_x, second : second + rows_z, third : third + rows_y]
        grand_quantity = grand_quantity + jnp.einsum(
            "dc,cxzy->dxzy",
            weights[:, :, first, second, third],
            window,
            preferred_element_type=jnp.float32,
        )
    return grand_quantity


def squares(remainder_grid):
    return lax.psum(jnp.sum(remainder_grid * remainder_grid, axis=(1, 2, 3)), ("xy", "gz"))[
        :, None, None, None
    ]


def local(image, filt, planted_colours, likelihoods, loss_slope):
    channels_here = image.shape[0]
    labels_here = likelihoods.shape[0]
    rows_x, rows_z, rows_y = (likelihoods.shape[1], likelihoods.shape[2], likelihoods.shape[3])
    lab_index = lax.axis_index("lab")
    own_filt = lax.dynamic_slice_in_dim(filt, lab_index * channels_here, channels_here, 1)
    image_edge = with_halo(image, (("xy", 1), ("gz", 2)), 1)
    own_wide = jnp.pad(image_edge, ((0, 0), (0, 0), (0, 0), (1, 1)))
    logits = lax.psum(
        correlate(own_filt, own_wide, rows_x, rows_z, rows_y).astype(jnp.bfloat16), "lab"
    ).astype(jnp.float32)
    xy_index = lax.axis_index("xy")
    gz_index = lax.axis_index("gz")
    xy_count = lax.axis_size("xy")
    gz_count = lax.axis_size("gz")
    shape = (rows_x, rows_z, rows_y)
    along_x = jnp.arange(rows_x, dtype=jnp.int32) + xy_index * rows_x < rows_x * xy_count - 1
    along_z = jnp.arange(rows_z, dtype=jnp.int32) + gz_index * rows_z < rows_z * gz_count - 1
    along_y = jnp.arange(rows_y, dtype=jnp.int32) < rows_y - 1
    edge_valid = jnp.stack(
        [
            jnp.broadcast_to(along_x[:, None, None], shape),
            jnp.broadcast_to(along_z[None, :, None], shape),
            jnp.broadcast_to(along_y[None, None, :], shape),
        ]
    ).astype(jnp.float32)
    squashed = jax.nn.sigmoid(logits)
    weight = (0.05 + squashed) * edge_valid
    below_x = passed_along(weight[0, -1:], "xy", 1)
    lower_x = jnp.concatenate([below_x, weight[0, :-1]], axis=0)
    below_z = passed_along(weight[1, :, -1:], "gz", 1)
    lower_z = jnp.concatenate([below_z, weight[1, :, :-1]], axis=1)
    lower_y = jnp.concatenate(
        [jnp.zeros((rows_x, rows_z, 1), jnp.float32), weight[2, :, :, :-1]], axis=2
    )
    class_count_overall = labels_here * lax.axis_size("lab")
    free_cell_flags = (planted_colours >= class_count_overall).astype(jnp.float32)[None]
    colours = lab_index * labels_here + jnp.arange(labels_here, dtype=jnp.int32)
    class_membership = (planted_colours[None] == colours[:, None, None, None]).astype(jnp.float32)
    entire_grid_state = free_cell_flags * likelihoods + class_membership
    adjoint = jnp.zeros_like(likelihoods)
    remainder_grid = free_cell_flags * loss_slope
    direction = remainder_grid
    norm_now = squares(remainder_grid)
    for count in range(ITERS):
        extended = with_halo(direction.astype(jnp.bfloat16), (("xy", 1), ("gz", 2)), 1).astype(
            direction.dtype
        )
        zeros_y = jnp.zeros(direction.shape[:3] + (1,), jnp.float32)
        upper_y = jnp.concatenate([direction[..., 1:], zeros_y], axis=3)
        under_y = jnp.concatenate([zeros_y, direction[..., :-1]], axis=3)
        grand_quantity = weight[0] * (direction - extended[:, 2:, 1:-1]) + lower_x * (
            direction - extended[:, :-2, 1:-1]
        )
        grand_quantity = (
            grand_quantity
            + weight[1] * (direction - extended[:, 1:-1, 2:])
            + lower_z * (direction - extended[:, 1:-1, :-2])
        )
        grand_quantity = (
            grand_quantity + weight[2] * (direction - upper_y) + lower_y * (direction - under_y)
        )
        picture_pixels_flat = free_cell_flags * grand_quantity
        curve = lax.psum(jnp.sum(direction * picture_pixels_flat, axis=(1, 2, 3)), ("xy", "gz"))
        alpha = norm_now / curve[:, None, None, None]
        adjoint = adjoint + alpha * direction
        remainder_grid = remainder_grid - alpha * picture_pixels_flat
        norm_next = squares(remainder_grid)
        direction = remainder_grid + norm_next / norm_now * direction
        norm_now = norm_next
    field_pair = jnp.concatenate([adjoint, entire_grid_state], axis=0)
    above_x = passed_along(field_pair[:, :1].astype(jnp.bfloat16), "xy", -1).astype(jnp.float32)
    next_x = jnp.concatenate([field_pair[:, 1:], above_x], axis=1)
    above_z = passed_along(field_pair[:, :, :1], "gz", -1)
    next_z = jnp.concatenate([field_pair[:, :, 1:], above_z], axis=2)
    next_y = jnp.concatenate(
        [field_pair[..., 1:], jnp.zeros(field_pair.shape[:3] + (1,), jnp.float32)], axis=3
    )
    partial_grads = []
    for neighbour in (next_x, next_z, next_y):
        change = field_pair - neighbour
        partial_grads.append(-jnp.sum(change[:labels_here] * change[labels_here:], axis=0))
    edge_grad = lax.psum(jnp.stack(partial_grads), "lab")
    logit_grad = (edge_grad * squashed * (1.0 - squashed) * edge_valid).astype(jnp.bfloat16)
    grad_edge = with_halo(logit_grad, (("xy", 1), ("gz", 2)), 1)
    grad_wide = jnp.pad(grad_edge, ((0, 0), (0, 0), (0, 0), (1, 1)))
    grad_image = jnp.zeros((channels_here, rows_x, rows_z, rows_y), jnp.float32)
    filter_terms = []
    for first, second, third in offsets():
        window = grad_wide[
            :,
            2 - first : 2 - first + rows_x,
            2 - second : 2 - second + rows_z,
            2 - third : 2 - third + rows_y,
        ]
        grad_image = grad_image + jnp.einsum(
            "dc,dxzy->cxzy",
            own_filt[:, :, first, second, third],
            window,
            preferred_element_type=jnp.float32,
        )
        image_window = own_wide[
            :, first : first + rows_x, second : second + rows_z, third : third + rows_y
        ]
        filter_terms.append(
            jnp.einsum(
                "dxzy,cxzy->dc", logit_grad, image_window, preferred_element_type=jnp.float32
            )
        )
    filter_part = jnp.stack(filter_terms, axis=-1).reshape(3, channels_here, 3, 3, 3)
    grad_filter = lax.psum(filter_part, ("xy", "gz"))
    return (grad_image.astype(jnp.bfloat16), grad_filter)


def solution(mesh):
    return jax.shard_map(
        local,
        mesh=mesh,
        in_specs=(
            P("lab", ("crops", "xy"), "gz", None),
            P(),
            P(("crops", "xy"), "gz", None),
            P("lab", ("crops", "xy"), "gz", None),
            P("lab", ("crops", "xy"), "gz", None),
        ),
        out_specs=(P("lab", ("crops", "xy"), "gz", None), P("crops", "lab", None, None, None)),
        check_vma=False,
    )
```

profile of v0, /device:TPU:0, one launch (start us, length us, event | category | flops | bytes accessed | tf_op | source)
XLA Modules:
  0.0 312.0 jit_solution(1046695100650287679)
XLA Ops:
  9.7 5.6 %collective-permute-start = (bf16[8,1,32,128]{3,0,2,1:T(8,128)(2,1)S(1)}, bf16[8,1,32,128]{3,0,2,1:T(8,128)(2,1)S(1)}, u32[]{:S(2)}, u32[]{:S(2)}) collective-permute-start(bf16[8,1,32,128]{3,0,2,1:T(8,128)(2,1)S(1)} %get-tuple-element.42), channel_id=1, source_target_pairs={{0,4},{4,8},{8,12},{1,5},{5,9},{9,13},{2,6},{6,10},{10,14},{3,7},{... | collective-permute-start | bytes 196616 | tf_op jit(solution)/shard_map/ppermute | solution.py:17
  16.2 4.1 %collective-permute-start.4 = (bf16[4,1,32,128]{3,2,1,0:T(8,128)(2,1)S(1)}, bf16[4,1,32,128]{3,2,1,0:T(8,128)(2,1)S(1)}, u32[]{:S(2)}, u32[]{:S(2)}) collective-permute-start(bf16[4,1,32,128]{3,2,1,0:T(8,128)(2,1)S(1)} %get-tuple-element.59), channel_id=1, source_target_pairs={{0,4},{4,8},{8,12},{1,5},{5,9},{9,13},{2,6},{6,10},{10,14},{3,7},{... | collective-permute-start | bytes 98312 | tf_op jit(solution)/shard_map/ppermute | solution.py:17
  23.1 3.4 %collective-permute-start.2 = (bf16[8,6,1,128]{3,0,2,1:T(8,128)(2,1)S(1)}, bf16[8,6,1,128]{3,0,2,1:T(8,128)(2,1)S(1)}, u32[]{:S(2)}, u32[]{:S(2)}) collective-permute-start(bf16[8,6,1,128]{3,0,2,1:T(8,128)(2,1)S(1)} %get-tuple-element.30), channel_id=1, source_target_pairs={{0,2},{1,3},{4,6},{5,7},{8,10},{9,11},{12,14},{13,15},{16,18},{17,... | collective-permute-start | bytes 36872 | tf_op jit(solution)/shard_map/ppermute | solution.py:17
  27.8 4.5 %collective-permute-start.6 = (bf16[4,6,1,128]{3,2,1,0:T(2,128)(2,1)S(1)}, bf16[4,6,1,128]{3,2,1,0:T(2,128)(2,1)S(1)}, u32[]{:S(2)}, u32[]{:S(2)}) collective-permute-start(bf16[4,6,1,128]{3,2,1,0:T(2,128)(2,1)S(1)} %get-tuple-element.51), channel_id=1, source_target_pairs={{0,2},{1,3},{4,6},{5,7},{8,10},{9,11},{12,14},{13,15},{16,18},{17,... | collective-permute-start | bytes 18440 | tf_op jit(solution)/shard_map/ppermute | solution.py:17
  42.4 20.3 %all-reduce.14.cloned.1.call-done = bf16[3,4,32,128]{3,0,2,1:T(4,128)(2,1)} async-done(((bf16[3,4,32,128]{3,0,2,1:T(4,128)(2,1)}), bf16[3,4,32,128]{3,0,2,1:T(4,128)(2,1)}) %all-reduce.14.cloned.1.call-update) | async-done | bytes 98320 | tf_op jit(solution)/shard_map/psum | solution.py:65
  64.4 3.6 %collective-permute-start.9 = (f32[4,1,128]{2,0,1:T(4,128)S(1)}, f32[4,1,128]{2,0,1:T(4,128)S(1)}, u32[]{:S(2)}, u32[]{:S(2)}) collective-permute-start(f32[4,1,128]{2,0,1:T(4,128)S(1)} %bitcast.468), channel_id=1, source_target_pairs={{0,2},{1,3},{4,6},{5,7},{8,10},{9,11},{12,14},{13,15},{16,18},{17,... | collective-permute-start | bytes 6152 | tf_op jit(solution)/shard_map/ppermute | solution.py:29
  68.4 3.4 %collective-permute-start.8 = (f32[1,32,128]{2,1,0:T(8,128)S(1)}, f32[1,32,128]{2,1,0:T(8,128)S(1)}, u32[]{:S(2)}, u32[]{:S(2)}) collective-permute-start(f32[1,32,128]{2,1,0:T(8,128)S(1)} %bitcast.466), channel_id=1, source_target_pairs={{0,4},{4,8},{8,12},{1,5},{5,9},{9,13},{2,6},{6,10},{10,14},{3,7},{... | collective-permute-start | bytes 49160 | tf_op jit(solution)/shard_map/ppermute | solution.py:29
  73.8 20.1 %all-reduce.10 = (f32[4]{0:T(128)S(1)}, f32[4]{0:T(128)S(1)}) all-reduce(f32[4]{0:T(128)S(1)} %get-tuple-element.13, f32[4]{0:T(128)S(1)} %get-tuple-element.12), channel_id=1, replica_groups=mesh['crops'=2,'xy'=4,'gz'=2,'lab'=2] {'xy','gz'}, use_global_device_ids=true, to_apply=%region_1.2 | all-reduce | flops 8 | bytes 64 | tf_op jit(solution)/shard_map/psum | solution.py:52
  94.1 17.2 %psum.66 = f32[4]{0:T(128)S(1)} all-reduce(f32[4]{0:T(128)S(1)} %get-tuple-element.22), channel_id=1, replica_groups=mesh['crops'=2,'xy'=4,'gz'=2,'lab'=2] {'xy','gz'}, use_global_device_ids=true, to_apply=%region_6.7 | all-reduce | flops 4 | bytes 32 | tf_op jit(solution)/shard_map/psum | solution.py:52
  114.9 4.2 %collective-permute-done.11 = bf16[4,1,32,128]{3,2,1,0:T(8,128)(2,1)S(1)} collective-permute-done((bf16[4,1,32,128]{3,2,1,0:T(8,128)(2,1)S(1)}, bf16[4,1,32,128]{3,2,1,0:T(8,128)(2,1)S(1)}, u32[]{:S(2)}, u32[]{:S(2)}) %collective-permute-start.11) | collective-permute-done | bytes 32800 | tf_op jit(solution)/shard_map/ppermute | solution.py:19
  119.1 3.8 %collective-permute-start.12 = (bf16[4,6,1,128]{3,2,1,0:T(2,128)(2,1)S(1)}, bf16[4,6,1,128]{3,2,1,0:T(2,128)(2,1)S(1)}, u32[]{:S(2)}, u32[]{:S(2)}) collective-permute-start(bf16[4,6,1,128]{3,2,1,0:T(2,128)(2,1)S(1)} %get-tuple-element.49), channel_id=1, source_target_pairs={{0,2},{1,3},{4,6},{5,7},{8,10},{9,11},{12,14},{13,15},{16,18},{17,... | collective-permute-start | bytes 18440 | tf_op jit(solution)/shard_map/ppermute | solution.py:17
  124.4 4.1 %collective-permute-done.13 = bf16[4,6,1,128]{3,2,1,0:T(2,128)(2,1)S(1)} collective-permute-done((bf16[4,6,1,128]{3,2,1,0:T(2,128)(2,1)S(1)}, bf16[4,6,1,128]{3,2,1,0:T(2,128)(2,1)S(1)}, u32[]{:S(2)}, u32[]{:S(2)}) %collective-permute-start.13) | collective-permute-done | bytes 6176 | tf_op jit(solution)/shard_map/ppermute | solution.py:19
  129.6 17.3 %psum.67 = f32[4]{0:T(128)S(1)} all-reduce(f32[4]{0:T(128)} %get-tuple-element.18), channel_id=1, replica_groups=mesh['crops'=2,'xy'=4,'gz'=2,'lab'=2] {'xy','gz'}, use_global_device_ids=true, to_apply=%region_8.9 | all-reduce | flops 4 | bytes 32 | tf_op jit(solution)/shard_map/psum | solution.py:120
  147.7 19.1 %psum.68 = f32[4]{0:T(128)S(1)} all-reduce(f32[4]{0:T(128)S(1)} %multiply_reduce_fusion), channel_id=1, replica_groups=mesh['crops'=2,'xy'=4,'gz'=2,'lab'=2] {'xy','gz'}, use_global_device_ids=true, to_apply=%region_10.11 | all-reduce | flops 4 | bytes 32 | tf_op jit(solution)/shard_map/psum | solution.py:52
  171.7 4.2 %collective-permute-done.15 = bf16[4,1,32,128]{3,2,1,0:T(8,128)(2,1)S(1)} collective-permute-done((bf16[4,1,32,128]{3,2,1,0:T(8,128)(2,1)S(1)}, bf16[4,1,32,128]{3,2,1,0:T(8,128)(2,1)S(1)}, u32[]{:S(2)}, u32[]{:S(2)}) %collective-permute-start.15) | collective-permute-done | bytes 32800 | tf_op jit(solution)/shard_map/ppermute | solution.py:19
  176.0 2.0 collective-permute-start.16
  179.4 4.1 %collective-permute-done.17 = bf16[4,6,1,128]{3,2,1,0:T(2,128)(2,1)S(1)} collective-permute-done((bf16[4,6,1,128]{3,2,1,0:T(2,128)(2,1)S(1)}, bf16[4,6,1,128]{3,2,1,0:T(2,128)(2,1)S(1)}, u32[]{:S(2)}, u32[]{:S(2)}) %collective-permute-start.17) | collective-permute-done | bytes 6176 | tf_op jit(solution)/shard_map/ppermute | solution.py:19
  184.1 17.2 %psum.69 = f32[4]{0:T(128)S(1)} all-reduce(f32[4]{0:T(128)S(1)} %fusion.71), channel_id=1, replica_groups=mesh['crops'=2,'xy'=4,'gz'=2,'lab'=2] {'xy','gz'}, use_global_device_ids=true, to_apply=%region_12.13 | all-reduce | flops 4 | bytes 32 | tf_op jit(solution)/shard_map/psum | solution.py:120
  204.5 4.6 %collective-permute-done.18 = bf16[8,1,32,128]{3,2,1,0:T(8,128)(2,1)S(1)} collective-permute-done((bf16[8,1,32,128]{3,2,1,0:T(8,128)(2,1)S(1)}, bf16[8,1,32,128]{3,2,1,0:T(8,128)(2,1)S(1)}, u32[]{:S(2)}, u32[]{:S(2)}) %collective-permute-start.18) | collective-permute-done | bytes 65568 | tf_op jit(solution)/shard_map/ppermute | solution.py:29
  210.6 17.7 %all-reduce.16.cloned.1.call-done = f32[3,4,32,128]{3,0,2,1:T(4,128)} async-done(((f32[3,4,32,128]{3,0,2,1:T(4,128)}), f32[3,4,32,128]{3,0,2,1:T(4,128)}) %all-reduce.16.cloned.1.call-update) | async-done | bytes 196624 | tf_op jit(solution)/shard_map/psum | solution.py:139
  237.9 3.7 %collective-permute-start.20 = (bf16[3,1,32,128]{3,0,2,1:T(4,128)(2,1)S(1)}, bf16[3,1,32,128]{3,0,2,1:T(4,128)(2,1)S(1)}, u32[]{:S(2)}, u32[]{:S(2)}) collective-permute-start(bf16[3,1,32,128]{3,0,2,1:T(4,128)(2,1)S(1)} %get-tuple-element.53), channel_id=1, source_target_pairs={{0,4},{4,8},{8,12},{1,5},{5,9},{9,13},{2,6},{6,10},{10,14},{3,7},{... | collective-permute-start | bytes 73736 | tf_op jit(solution)/shard_map/ppermute | solution.py:17
  243.1 4.2 %collective-permute-done.21 = bf16[3,1,32,128]{3,0,2,1:T(4,128)(2,1)S(1)} collective-permute-done((bf16[3,1,32,128]{3,0,2,1:T(4,128)(2,1)S(1)}, bf16[3,1,32,128]{3,0,2,1:T(4,128)(2,1)S(1)}, u32[]{:S(2)}, u32[]{:S(2)}) %collective-permute-start.21) | collective-permute-done | bytes 24608 | tf_op jit(solution)/shard_map/ppermute | solution.py:19
  247.4 3.4 %collective-permute-start.22 = (bf16[3,6,1,128]{3,0,2,1:T(4,128)(2,1)S(1)}, bf16[3,6,1,128]{3,0,2,1:T(4,128)(2,1)S(1)}, u32[]{:S(2)}, u32[]{:S(2)}) collective-permute-start(bf16[3,6,1,128]{3,0,2,1:T(4,128)(2,1)S(1)} %get-tuple-element.45), channel_id=1, source_target_pairs={{0,2},{1,3},{4,6},{5,7},{8,10},{9,11},{12,14},{13,15},{16,18},{17,... | collective-permute-start | bytes 13832 | tf_op jit(solution)/shard_map/ppermute | solution.py:17
  252.4 37.5 %psum.71 = f32[3,8,3,3,3]{1,4,3,2,0:T(4,128)} all-reduce(f32[3,8,3,3,3]{1,4,3,2,0:T(4,128)S(1)} %copy.170), channel_id=1, replica_groups=mesh['crops'=2,'xy'=4,'gz'=2,'lab'=2] {'xy','gz'}, use_global_device_ids=true, to_apply=%region_17.18 | all-reduce | flops 648 | bytes 5184 | tf_op jit(solution)/shard_map/psum | solution.py:167
  (366 shorter events, 66.9 us)
Async XLA Ops:
  7.2 55.5 %all-reduce.14.cloned.1.call-start = ((), (), s32[]{:S(2)}) async-start(), calls=%async_computation | async-start | bytes 262144 | tf_op jit(solution)/shard_map/psum | solution.py:65
  8.4 14.6 %collective-permute-start.1 = (bf16[8,1,32,128]{3,0,2,1:T(8,128)(2,1)S(1)}, bf16[8,1,32,128]{3,0,2,1:T(8,128)(2,1)S(1)}, u32[]{:S(2)}, u32[]{:S(2)}) collective-permute-start(bf16[8,1,32,128]{3,0,2,1:T(8,128)(2,1)S(1)} %get-tuple-element.41), channel_id=1, source_target_pairs={{4,0},{8,4},{12,8},{5,1},{9,5},{13,9},{6,2},{10,6},{14,10},{7,3},{... | collective-permute-start | bytes 196616 | tf_op jit(solution)/shard_map/ppermute | solution.py:19
  9.7 13.1 %collective-permute-start = (bf16[8,1,32,128]{3,0,2,1:T(8,128)(2,1)S(1)}, bf16[8,1,32,128]{3,0,2,1:T(8,128)(2,1)S(1)}, u32[]{:S(2)}, u32[]{:S(2)}) collective-permute-start(bf16[8,1,32,128]{3,0,2,1:T(8,128)(2,1)S(1)} %get-tuple-element.42), channel_id=1, source_target_pairs={{0,4},{4,8},{8,12},{1,5},{5,9},{9,13},{2,6},{6,10},{10,14},{3,7},{... | collective-permute-start | bytes 196616 | tf_op jit(solution)/shard_map/ppermute | solution.py:17
  16.2 11.6 %collective-permute-start.4 = (bf16[4,1,32,128]{3,2,1,0:T(8,128)(2,1)S(1)}, bf16[4,1,32,128]{3,2,1,0:T(8,128)(2,1)S(1)}, u32[]{:S(2)}, u32[]{:S(2)}) collective-permute-start(bf16[4,1,32,128]{3,2,1,0:T(8,128)(2,1)S(1)} %get-tuple-element.59), channel_id=1, source_target_pairs={{0,4},{4,8},{8,12},{1,5},{5,9},{9,13},{2,6},{6,10},{10,14},{3,7},{... | collective-permute-start | bytes 98312 | tf_op jit(solution)/shard_map/ppermute | solution.py:17
  20.3 7.5 %collective-permute-start.5 = (bf16[4,1,32,128]{3,2,1,0:T(8,128)(2,1)S(1)}, bf16[4,1,32,128]{3,2,1,0:T(8,128)(2,1)S(1)}, u32[]{:S(2)}, u32[]{:S(2)}) collective-permute-start(bf16[4,1,32,128]{3,2,1,0:T(8,128)(2,1)S(1)} %get-tuple-element.60), channel_id=1, source_target_pairs={{4,0},{8,4},{12,8},{5,1},{9,5},{13,9},{6,2},{10,6},{14,10},{7,3},{... | collective-permute-start | bytes 98312 | tf_op jit(solution)/shard_map/ppermute | solution.py:19
  23.1 10.6 %collective-permute-start.2 = (bf16[8,6,1,128]{3,0,2,1:T(8,128)(2,1)S(1)}, bf16[8,6,1,128]{3,0,2,1:T(8,128)(2,1)S(1)}, u32[]{:S(2)}, u32[]{:S(2)}) collective-permute-start(bf16[8,6,1,128]{3,0,2,1:T(8,128)(2,1)S(1)} %get-tuple-element.30), channel_id=1, source_target_pairs={{0,2},{1,3},{4,6},{5,7},{8,10},{9,11},{12,14},{13,15},{16,18},{17,... | collective-permute-start | bytes 36872 | tf_op jit(solution)/shard_map/ppermute | solution.py:17
  26.5 7.2 %collective-permute-start.3 = (bf16[8,6,1,128]{3,0,2,1:T(8,128)(2,1)S(1)}, bf16[8,6,1,128]{3,0,2,1:T(8,128)(2,1)S(1)}, u32[]{:S(2)}, u32[]{:S(2)}) collective-permute-start(bf16[8,6,1,128]{3,0,2,1:T(8,128)(2,1)S(1)} %get-tuple-element.31), channel_id=1, source_target_pairs={{2,0},{3,1},{6,4},{7,5},{10,8},{11,9},{14,12},{15,13},{18,16},{19,... | collective-permute-start | bytes 36872 | tf_op jit(solution)/shard_map/ppermute | solution.py:19
  27.8 14.4 %collective-permute-start.6 = (bf16[4,6,1,128]{3,2,1,0:T(2,128)(2,1)S(1)}, bf16[4,6,1,128]{3,2,1,0:T(2,128)(2,1)S(1)}, u32[]{:S(2)}, u32[]{:S(2)}) collective-permute-start(bf16[4,6,1,128]{3,2,1,0:T(2,128)(2,1)S(1)} %get-tuple-element.51), channel_id=1, source_target_pairs={{0,2},{1,3},{4,6},{5,7},{8,10},{9,11},{12,14},{13,15},{16,18},{17,... | collective-permute-start | bytes 18440 | tf_op jit(solution)/shard_map/ppermute | solution.py:17
  32.4 9.8 %collective-permute-start.7 = (bf16[4,6,1,128]{3,2,1,0:T(2,128)(2,1)S(1)}, bf16[4,6,1,128]{3,2,1,0:T(2,128)(2,1)S(1)}, u32[]{:S(2)}, u32[]{:S(2)}) collective-permute-start(bf16[4,6,1,128]{3,2,1,0:T(2,128)(2,1)S(1)} %get-tuple-element.52), channel_id=1, source_target_pairs={{2,0},{3,1},{6,4},{7,5},{10,8},{11,9},{14,12},{15,13},{18,16},{19,... | collective-permute-start | bytes 18440 | tf_op jit(solution)/shard_map/ppermute | solution.py:19
  42.2 186.2 %all-reduce.16.cloned.1.call-start = ((), (), s32[]{:S(2)}) async-start(), calls=%async_computation.1 | async-start | bytes 524288 | tf_op jit(solution)/shard_map/psum | solution.py:139
  64.4 7.6 %collective-permute-start.9 = (f32[4,1,128]{2,0,1:T(4,128)S(1)}, f32[4,1,128]{2,0,1:T(4,128)S(1)}, u32[]{:S(2)}, u32[]{:S(2)}) collective-permute-start(f32[4,1,128]{2,0,1:T(4,128)S(1)} %bitcast.468), channel_id=1, source_target_pairs={{0,2},{1,3},{4,6},{5,7},{8,10},{9,11},{12,14},{13,15},{16,18},{17,... | collective-permute-start | bytes 6152 | tf_op jit(solution)/shard_map/ppermute | solution.py:29
  68.4 4.8 %collective-permute-start.8 = (f32[1,32,128]{2,1,0:T(8,128)S(1)}, f32[1,32,128]{2,1,0:T(8,128)S(1)}, u32[]{:S(2)}, u32[]{:S(2)}) collective-permute-start(f32[1,32,128]{2,1,0:T(8,128)S(1)} %bitcast.466), channel_id=1, source_target_pairs={{0,4},{4,8},{8,12},{1,5},{5,9},{9,13},{2,6},{6,10},{10,14},{3,7},{... | collective-permute-start | bytes 49160 | tf_op jit(solution)/shard_map/ppermute | solution.py:29
  113.3 5.8 %collective-permute-start.11 = (bf16[4,1,32,128]{3,2,1,0:T(8,128)(2,1)S(1)}, bf16[4,1,32,128]{3,2,1,0:T(8,128)(2,1)S(1)}, u32[]{:S(2)}, u32[]{:S(2)}) collective-permute-start(bf16[4,1,32,128]{3,2,1,0:T(8,128)(2,1)S(1)} %get-tuple-element.58), channel_id=1, source_target_pairs={{4,0},{8,4},{12,8},{5,1},{9,5},{13,9},{6,2},{10,6},{14,10},{7,3},{... | collective-permute-start | bytes 98312 | tf_op jit(solution)/shard_map/ppermute | solution.py:19
  119.1 5.3 %collective-permute-start.12 = (bf16[4,6,1,128]{3,2,1,0:T(2,128)(2,1)S(1)}, bf16[4,6,1,128]{3,2,1,0:T(2,128)(2,1)S(1)}, u32[]{:S(2)}, u32[]{:S(2)}) collective-permute-start(bf16[4,6,1,128]{3,2,1,0:T(2,128)(2,1)S(1)} %get-tuple-element.49), channel_id=1, source_target_pairs={{0,2},{1,3},{4,6},{5,7},{8,10},{9,11},{12,14},{13,15},{16,18},{17,... | collective-permute-start | bytes 18440 | tf_op jit(solution)/shard_map/ppermute | solution.py:17
  122.9 5.6 %collective-permute-start.13 = (bf16[4,6,1,128]{3,2,1,0:T(2,128)(2,1)S(1)}, bf16[4,6,1,128]{3,2,1,0:T(2,128)(2,1)S(1)}, u32[]{:S(2)}, u32[]{:S(2)}) collective-permute-start(bf16[4,6,1,128]{3,2,1,0:T(2,128)(2,1)S(1)} %get-tuple-element.50), channel_id=1, source_target_pairs={{2,0},{3,1},{6,4},{7,5},{10,8},{11,9},{14,12},{15,13},{18,16},{19,... | collective-permute-start | bytes 18440 | tf_op jit(solution)/shard_map/ppermute | solution.py:19
  170.1 5.8 %collective-permute-start.15 = (bf16[4,1,32,128]{3,2,1,0:T(8,128)(2,1)S(1)}, bf16[4,1,32,128]{3,2,1,0:T(8,128)(2,1)S(1)}, u32[]{:S(2)}, u32[]{:S(2)}) collective-permute-start(bf16[4,1,32,128]{3,2,1,0:T(8,128)(2,1)S(1)} %get-tuple-element.56), channel_id=1, source_target_pairs={{4,0},{8,4},{12,8},{5,1},{9,5},{13,9},{6,2},{10,6},{14,10},{7,3},{... | collective-permute-start | bytes 98312 | tf_op jit(solution)/shard_map/ppermute | solution.py:19
  176.0 3.5 %collective-permute-start.16 = (bf16[4,6,1,128]{3,2,1,0:T(2,128)(2,1)S(1)}, bf16[4,6,1,128]{3,2,1,0:T(2,128)(2,1)S(1)}, u32[]{:S(2)}, u32[]{:S(2)}) collective-permute-start(bf16[4,6,1,128]{3,2,1,0:T(2,128)(2,1)S(1)} %get-tuple-element.47), channel_id=1, source_target_pairs={{0,2},{1,3},{4,6},{5,7},{8,10},{9,11},{12,14},{13,15},{16,18},{17,... | collective-permute-start | bytes 18440 | tf_op jit(solution)/shard_map/ppermute | solution.py:17
  177.9 5.6 %collective-permute-start.17 = (bf16[4,6,1,128]{3,2,1,0:T(2,128)(2,1)S(1)}, bf16[4,6,1,128]{3,2,1,0:T(2,128)(2,1)S(1)}, u32[]{:S(2)}, u32[]{:S(2)}) collective-permute-start(bf16[4,6,1,128]{3,2,1,0:T(2,128)(2,1)S(1)} %get-tuple-element.48), channel_id=1, source_target_pairs={{2,0},{3,1},{6,4},{7,5},{10,8},{11,9},{14,12},{15,13},{18,16},{19,... | collective-permute-start | bytes 18440 | tf_op jit(solution)/shard_map/ppermute | solution.py:19
  201.7 7.5 %collective-permute-start.19 = (f32[8,4,1,128]{3,2,1,0:T(1,128)S(1)}, f32[8,4,1,128]{3,2,1,0:T(1,128)S(1)}, u32[]{:S(2)}, u32[]{:S(2)}) collective-permute-start(f32[8,4,1,128]{3,2,1,0:T(1,128)S(1)} %fusion.176), channel_id=1, source_target_pairs={{2,0},{3,1},{6,4},{7,5},{10,8},{11,9},{14,12},{15,13},{18,16},{19,... | collective-permute-start | bytes 49160 | tf_op jit(solution)/shard_map/ppermute | solution.py:29
  203.0 6.2 %collective-permute-start.18 = (bf16[8,1,32,128]{3,2,1,0:T(8,128)(2,1)S(1)}, bf16[8,1,32,128]{3,2,1,0:T(8,128)(2,1)S(1)}, u32[]{:S(2)}, u32[]{:S(2)}) collective-permute-start(bf16[8,1,32,128]{3,2,1,0:T(8,128)(2,1)S(1)} %fusion.141), channel_id=1, source_target_pairs={{4,0},{8,4},{12,8},{5,1},{9,5},{13,9},{6,2},{10,6},{14,10},{7,3},{... | collective-permute-start | bytes 196616 | tf_op jit(solution)/shard_map/ppermute | solution.py:29
  237.9 5.3 %collective-permute-start.20 = (bf16[3,1,32,128]{3,0,2,1:T(4,128)(2,1)S(1)}, bf16[3,1,32,128]{3,0,2,1:T(4,128)(2,1)S(1)}, u32[]{:S(2)}, u32[]{:S(2)}) collective-permute-start(bf16[3,1,32,128]{3,0,2,1:T(4,128)(2,1)S(1)} %get-tuple-element.53), channel_id=1, source_target_pairs={{0,4},{4,8},{8,12},{1,5},{5,9},{9,13},{2,6},{6,10},{10,14},{3,7},{... | collective-permute-start | bytes 73736 | tf_op jit(solution)/shard_map/ppermute | solution.py:17
  241.5 5.8 %collective-permute-start.21 = (bf16[3,1,32,128]{3,0,2,1:T(4,128)(2,1)S(1)}, bf16[3,1,32,128]{3,0,2,1:T(4,128)(2,1)S(1)}, u32[]{:S(2)}, u32[]{:S(2)}) collective-permute-start(bf16[3,1,32,128]{3,0,2,1:T(4,128)(2,1)S(1)} %get-tuple-element.54), channel_id=1, source_target_pairs={{4,0},{8,4},{12,8},{5,1},{9,5},{13,9},{6,2},{10,6},{14,10},{7,3},{... | collective-permute-start | bytes 73736 | tf_op jit(solution)/shard_map/ppermute | solution.py:19
  247.4 42.6 %collective-permute-start.22 = (bf16[3,6,1,128]{3,0,2,1:T(4,128)(2,1)S(1)}, bf16[3,6,1,128]{3,0,2,1:T(4,128)(2,1)S(1)}, u32[]{:S(2)}, u32[]{:S(2)}) collective-permute-start(bf16[3,6,1,128]{3,0,2,1:T(4,128)(2,1)S(1)} %get-tuple-element.45), channel_id=1, source_target_pairs={{0,2},{1,3},{4,6},{5,7},{8,10},{9,11},{12,14},{13,15},{16,18},{17,... | collective-permute-start | bytes 13832 | tf_op jit(solution)/shard_map/ppermute | solution.py:17
  250.7 39.2 %collective-permute-start.23 = (bf16[3,6,1,128]{3,0,2,1:T(4,128)(2,1)S(1)}, bf16[3,6,1,128]{3,0,2,1:T(4,128)(2,1)S(1)}, u32[]{:S(2)}, u32[]{:S(2)}) collective-permute-start(bf16[3,6,1,128]{3,0,2,1:T(4,128)(2,1)S(1)} %get-tuple-element.46), channel_id=1, source_target_pairs={{2,0},{3,1},{6,4},{7,5},{10,8},{11,9},{14,12},{15,13},{18,16},{19,... | collective-permute-start | bytes 13832 | tf_op jit(solution)/shard_map/ppermute | solution.py:19
  (90 other events, 802.6 us)
Sparse Core Ops, SparseCore 0:
  42.3 20.3 all-reduce.13
  210.8 17.5 all-reduce.15
where the time goes:
time: 313 us; the launch traced here: 312 us
  blocking collectives  128 us (41%)
  waiting for transfers between devices  65.5 us (21%)
  starting transfers between devices  55.7 us (18%)
  matrix products  23.8 us (8%)
  between operations  15.9 us (5%)
  local copies, waits for them, and re-layouts  11.5 us (4%)
  other arithmetic  11.3 us (4%)
    psum x3, blocking collectives, squares(): lax.psum(jnp.sum(remainder_grid * remainder_grid, axis=(1, 2, 3)), ('xy',...  56.4 us
    psum x1, blocking collectives, local(): grad_filter = lax.psum(filter_part, ('xy', 'gz'))  37.5 us
    psum x2, blocking collectives, local(): lax.psum(jnp.sum(direction * picture_pixels_flat, axis=(1, 2, 3)), ('xy',...  34.5 us
    ppermute x10, starting transfers between devices, with_halo(): lax.ppermute(tail, axis, [(i, (i + 1) % count) for i in range(ends)])  32.9 us
    ppermute x10, waiting for transfers between devices, with_halo(): lax.ppermute(head, axis, [((i + 1) % count, i) for i in range(ends)])  20.9 us
    psum x1, waiting for transfers between devices, local(): lax.psum(correlate(own_filt, own_wide, rows_x, rows_z, rows_y).astype(jnp...  20.3 us
    psum x1, waiting for transfers between devices, local(): edge_grad = lax.psum(jnp.stack(partial_grads), 'lab')  17.7 us
    ppermute x10, starting transfers between devices, with_halo(): lax.ppermute(head, axis, [((i + 1) % count, i) for i in range(ends)])  12.9 us
  transfers between devices with their start and end apart: 26, of which 11 were waited for; matrix products, arithmetic and copies ran while one was open for 4% of the time, Pallas kernels for 0%

commit v1 on v0

--- a/solution.py
+++ b/solution.py
@@ -4,6 +4,11 @@
 from jax.sharding import PartitionSpec as P
 
 ITERS = 3
+
+
+def by_each_axis(array, axis_one, axis_two):
+    partial = lax.psum(array, axis_one)
+    return lax.psum(partial, axis_two)
 
 
 def with_halo(cells, sides, width):
@@ -49,7 +54,7 @@
 
 
 def squares(remainder_grid):
-    return lax.psum(jnp.sum(remainder_grid * remainder_grid, axis=(1, 2, 3)), ("xy", "gz"))[
+    return by_each_axis(jnp.sum(remainder_grid * remainder_grid, axis=(1, 2, 3)), "gz", "xy")[
         :, None, None, None
     ]
 

time: 313 us -> 323 us (1.032)
  blocking collectives: 128 us -> 135 us
    psum x2 -> x3, blocking collectives: 34.5 us -> 55 us  [local(): lax.psum(jnp.sum(direction * picture_pixels_flat, axis=(1, 2, 3)), ('xy',...]
    psum x3 -> x6, blocking collectives: 56.4 us -> 42.4 us  [the longest x3 27.6 us: by_each_axis(): return lax.psum(partial, axis_two)]
  transfers between devices with their start and end apart: 26 -> 26, of which waited for: 11 -> 11; matrix products, arithmetic and copies ran while one was open for 4% -> 3% of each run, Pallas kernels for 0% -> 0%
where the time goes in v1:
time: 323 us; the launch traced here: 322 us
  blocking collectives  135 us (42%)
  waiting for transfers between devices  65.6 us (20%)
  starting transfers between devices  58.9 us (18%)
  matrix products  23.8 us (7%)
  between operations  15.9 us (5%)
  local copies, waits for them, and re-layouts  11.5 us (4%)
  other arithmetic  11.3 us (3%)
    psum x3, blocking collectives, local(): lax.psum(jnp.sum(direction * picture_pixels_flat, axis=(1, 2, 3)), ('xy',...  55 us
    psum x1, blocking collectives, local(): grad_filter = lax.psum(filter_part, ('xy', 'gz'))  37.5 us
    ppermute x10, starting transfers between devices, with_halo(): lax.ppermute(tail, axis, [(i, (i + 1) % count) for i in range(ends)])  36.1 us
    psum x3, blocking collectives, by_each_axis(): return lax.psum(partial, axis_two)  27.6 us
    ppermute x10, waiting for transfers between devices, with_halo(): lax.ppermute(head, axis, [((i + 1) % count, i) for i in range(ends)])  20.9 us
    psum x1, waiting for transfers between devices, local(): lax.psum(correlate(own_filt, own_wide, rows_x, rows_z, rows_y).astype(jnp...  20.3 us
    psum x1, waiting for transfers between devices, local(): edge_grad = lax.psum(jnp.stack(partial_grads), 'lab')  17.7 us
    psum x3, blocking collectives, by_each_axis(): partial = lax.psum(array, axis_one)  14.8 us
  transfers between devices with their start and end apart: 26, of which 11 were waited for; matrix products, arithmetic and copies ran while one was open for 3% of the time, Pallas kernels for 0%

profile of v1, /device:TPU:0, one launch (start us, length us, event | category | flops | bytes accessed | tf_op | source)
XLA Modules:
  0.0 321.9 jit_solution(2962563963353542698)
XLA Ops:
  9.7 5.6 %collective-permute-start = (bf16[8,1,32,128]{3,0,2,1:T(8,128)(2,1)S(1)}, bf16[8,1,32,128]{3,0,2,1:T(8,128)(2,1)S(1)}, u32[]{:S(2)}, u32[]{:S(2)}) collective-permute-start(bf16[8,1,32,128]{3,0,2,1:T(8,128)(2,1)S(1)} %get-tuple-element.40), channel_id=1, source_target_pairs={{0,4},{4,8},{8,12},{1,5},{5,9},{9,13},{2,6},{6,10},{10,14},{3,7},{... | collective-permute-start | bytes 196616 | tf_op jit(solution)/shard_map/ppermute | solution.py:22
  16.2 4.1 %collective-permute-start.4 = (bf16[4,1,32,128]{3,2,1,0:T(8,128)(2,1)S(1)}, bf16[4,1,32,128]{3,2,1,0:T(8,128)(2,1)S(1)}, u32[]{:S(2)}, u32[]{:S(2)}) collective-permute-start(bf16[4,1,32,128]{3,2,1,0:T(8,128)(2,1)S(1)} %get-tuple-element.57), channel_id=1, source_target_pairs={{0,4},{4,8},{8,12},{1,5},{5,9},{9,13},{2,6},{6,10},{10,14},{3,7},{... | collective-permute-start | bytes 98312 | tf_op jit(solution)/shard_map/ppermute | solution.py:22
  27.8 4.5 %collective-permute-start.6 = (bf16[4,6,1,128]{3,2,1,0:T(2,128)(2,1)S(1)}, bf16[4,6,1,128]{3,2,1,0:T(2,128)(2,1)S(1)}, u32[]{:S(2)}, u32[]{:S(2)}) collective-permute-start(bf16[4,6,1,128]{3,2,1,0:T(2,128)(2,1)S(1)} %get-tuple-element.49), channel_id=1, source_target_pairs={{0,2},{1,3},{4,6},{5,7},{8,10},{9,11},{12,14},{13,15},{16,18},{17,... | collective-permute-start | bytes 18440 | tf_op jit(solution)/shard_map/ppermute | solution.py:22
  42.4 20.3 %all-reduce.13.cloned.1.call-done = bf16[3,4,32,128]{3,0,2,1:T(4,128)(2,1)} async-done(((bf16[3,4,32,128]{3,0,2,1:T(4,128)(2,1)}), bf16[3,4,32,128]{3,0,2,1:T(4,128)(2,1)}) %all-reduce.13.cloned.1.call-update) | async-done | bytes 98320 | tf_op jit(solution)/shard_map/psum | solution.py:70
  64.4 3.6 %collective-permute-start.9 = (f32[4,1,128]{2,0,1:T(4,128)S(1)}, f32[4,1,128]{2,0,1:T(4,128)S(1)}, u32[]{:S(2)}, u32[]{:S(2)}) collective-permute-start(f32[4,1,128]{2,0,1:T(4,128)S(1)} %bitcast.468), channel_id=1, source_target_pairs={{0,2},{1,3},{4,6},{5,7},{8,10},{9,11},{12,14},{13,15},{16,18},{17,... | collective-permute-start | bytes 6152 | tf_op jit(solution)/shard_map/ppermute | solution.py:34
  73.8 4.9 %psum.84 = f32[4]{0:T(128)S(1)} all-reduce(f32[4]{0:T(128)S(1)} %get-tuple-element.13), channel_id=1, replica_groups=mesh['crops'=2,'xy'=4,'gz'=2,'lab'=2] {'gz'}, use_global_device_ids=true, to_apply=%region_1.2 | all-reduce | flops 4 | bytes 32 | tf_op jit(solution)/shard_map/psum | solution.py:10
  78.8 20.7 %psum.87 = f32[4]{0:T(128)S(1)} all-reduce(f32[4]{0:T(128)S(1)} %get-tuple-element.12), channel_id=1, replica_groups=mesh['crops'=2,'xy'=4,'gz'=2,'lab'=2] {'xy','gz'}, use_global_device_ids=true, to_apply=%region_5.6 | all-reduce | flops 4 | bytes 32 | tf_op jit(solution)/shard_map/psum | solution.py:125
  99.4 8.4 %psum.85 = f32[4]{0:T(128)S(1)} all-reduce(f32[4]{0:T(128)S(1)} %psum.84), channel_id=1, replica_groups=mesh['crops'=2,'xy'=4,'gz'=2,'lab'=2] {'xy'}, use_global_device_ids=true, to_apply=%region_2.3 | all-reduce | flops 4 | bytes 32 | tf_op jit(solution)/shard_map/psum | solution.py:11
  108.0 4.9 %psum.88 = f32[4]{0:T(128)S(1)} all-reduce(f32[4]{0:T(128)S(1)} %get-tuple-element.20), channel_id=1, replica_groups=mesh['crops'=2,'xy'=4,'gz'=2,'lab'=2] {'gz'}, use_global_device_ids=true, to_apply=%region_7.8 | all-reduce | flops 4 | bytes 32 | tf_op jit(solution)/shard_map/psum | solution.py:10
  112.9 10.3 %psum.89 = f32[4]{0:T(128)S(1)} all-reduce(f32[4]{0:T(128)S(1)} %psum.88), channel_id=1, replica_groups=mesh['crops'=2,'xy'=4,'gz'=2,'lab'=2] {'xy'}, use_global_device_ids=true, to_apply=%region_8.9 | all-reduce | flops 4 | bytes 32 | tf_op jit(solution)/shard_map/psum | solution.py:11
  127.4 4.2 %collective-permute-done.11 = bf16[4,1,32,128]{3,2,1,0:T(8,128)(2,1)S(1)} collective-permute-done((bf16[4,1,32,128]{3,2,1,0:T(8,128)(2,1)S(1)}, bf16[4,1,32,128]{3,2,1,0:T(8,128)(2,1)S(1)}, u32[]{:S(2)}, u32[]{:S(2)}) %collective-permute-start.11) | collective-permute-done | bytes 32800 | tf_op jit(solution)/shard_map/ppermute | solution.py:24
  135.5 4.1 %collective-permute-done.13 = bf16[4,6,1,128]{3,2,1,0:T(2,128)(2,1)S(1)} collective-permute-done((bf16[4,6,1,128]{3,2,1,0:T(2,128)(2,1)S(1)}, bf16[4,6,1,128]{3,2,1,0:T(2,128)(2,1)S(1)}, u32[]{:S(2)}, u32[]{:S(2)}) %collective-permute-start.13) | collective-permute-done | bytes 6176 | tf_op jit(solution)/shard_map/ppermute | solution.py:24
  140.7 17.2 %psum.90 = f32[4]{0:T(128)S(1)} all-reduce(f32[4]{0:T(128)} %get-tuple-element.16), channel_id=1, replica_groups=mesh['crops'=2,'xy'=4,'gz'=2,'lab'=2] {'xy','gz'}, use_global_device_ids=true, to_apply=%region_10.11 | all-reduce | flops 4 | bytes 32 | tf_op jit(solution)/shard_map/psum | solution.py:125
  158.8 4.9 %psum.91 = f32[4]{0:T(128)S(1)} all-reduce(f32[4]{0:T(128)S(1)} %multiply_reduce_fusion), channel_id=1, replica_groups=mesh['crops'=2,'xy'=4,'gz'=2,'lab'=2] {'gz'}, use_global_device_ids=true, to_apply=%region_12.13 | all-reduce | flops 4 | bytes 32 | tf_op jit(solution)/shard_map/psum | solution.py:10
  163.7 8.9 %psum.92 = f32[4]{0:T(128)S(1)} all-reduce(f32[4]{0:T(128)S(1)} %psum.91), channel_id=1, replica_groups=mesh['crops'=2,'xy'=4,'gz'=2,'lab'=2] {'xy'}, use_global_device_ids=true, to_apply=%region_13.14 | all-reduce | flops 4 | bytes 32 | tf_op jit(solution)/shard_map/psum | solution.py:11
  179.5 4.2 %collective-permute-done.15 = bf16[4,1,32,128]{3,2,1,0:T(8,128)(2,1)S(1)} collective-permute-done((bf16[4,1,32,128]{3,2,1,0:T(8,128)(2,1)S(1)}, bf16[4,1,32,128]{3,2,1,0:T(8,128)(2,1)S(1)}, u32[]{:S(2)}, u32[]{:S(2)}) %collective-permute-start.15) | collective-permute-done | bytes 32800 | tf_op jit(solution)/shard_map/ppermute | solution.py:24
  183.8 3.9 %collective-permute-start.16 = (bf16[4,6,1,128]{3,2,1,0:T(2,128)(2,1)S(1)}, bf16[4,6,1,128]{3,2,1,0:T(2,128)(2,1)S(1)}, u32[]{:S(2)}, u32[]{:S(2)}) collective-permute-start(bf16[4,6,1,128]{3,2,1,0:T(2,128)(2,1)S(1)} %get-tuple-element.45), channel_id=1, source_target_pairs={{0,2},{1,3},{4,6},{5,7},{8,10},{9,11},{12,14},{13,15},{16,18},{17,... | collective-permute-start | bytes 18440 | tf_op jit(solution)/shard_map/ppermute | solution.py:22
  189.2 4.1 %collective-permute-done.17 = bf16[4,6,1,128]{3,2,1,0:T(2,128)(2,1)S(1)} collective-permute-done((bf16[4,6,1,128]{3,2,1,0:T(2,128)(2,1)S(1)}, bf16[4,6,1,128]{3,2,1,0:T(2,128)(2,1)S(1)}, u32[]{:S(2)}, u32[]{:S(2)}) %collective-permute-start.17) | collective-permute-done | bytes 6176 | tf_op jit(solution)/shard_map/ppermute | solution.py:24
  193.9 17.1 %psum.93 = f32[4]{0:T(128)S(1)} all-reduce(f32[4]{0:T(128)S(1)} %fusion.71), channel_id=1, replica_groups=mesh['crops'=2,'xy'=4,'gz'=2,'lab'=2] {'xy','gz'}, use_global_device_ids=true, to_apply=%region_15.16 | all-reduce | flops 4 | bytes 32 | tf_op jit(solution)/shard_map/psum | solution.py:125
  214.3 4.8 %collective-permute-done.18 = bf16[8,1,32,128]{3,2,1,0:T(8,128)(2,1)S(1)} collective-permute-done((bf16[8,1,32,128]{3,2,1,0:T(8,128)(2,1)S(1)}, bf16[8,1,32,128]{3,2,1,0:T(8,128)(2,1)S(1)}, u32[]{:S(2)}, u32[]{:S(2)}) %collective-permute-start.18) | collective-permute-done | bytes 65568 | tf_op jit(solution)/shard_map/ppermute | solution.py:34
  220.5 17.7 %all-reduce.15.cloned.1.call-done = f32[3,4,32,128]{3,0,2,1:T(4,128)} async-done(((f32[3,4,32,128]{3,0,2,1:T(4,128)}), f32[3,4,32,128]{3,0,2,1:T(4,128)}) %all-reduce.15.cloned.1.call-update) | async-done | bytes 196624 | tf_op jit(solution)/shard_map/psum | solution.py:144
  247.8 3.7 %collective-permute-start.20 = (bf16[3,1,32,128]{3,0,2,1:T(4,128)(2,1)S(1)}, bf16[3,1,32,128]{3,0,2,1:T(4,128)(2,1)S(1)}, u32[]{:S(2)}, u32[]{:S(2)}) collective-permute-start(bf16[3,1,32,128]{3,0,2,1:T(4,128)(2,1)S(1)} %get-tuple-element.51), channel_id=1, source_target_pairs={{0,4},{4,8},{8,12},{1,5},{5,9},{9,13},{2,6},{6,10},{10,14},{3,7},{... | collective-permute-start | bytes 73736 | tf_op jit(solution)/shard_map/ppermute | solution.py:22
  253.0 4.2 %collective-permute-done.21 = bf16[3,1,32,128]{3,0,2,1:T(4,128)(2,1)S(1)} collective-permute-done((bf16[3,1,32,128]{3,0,2,1:T(4,128)(2,1)S(1)}, bf16[3,1,32,128]{3,0,2,1:T(4,128)(2,1)S(1)}, u32[]{:S(2)}, u32[]{:S(2)}) %collective-permute-start.21) | collective-permute-done | bytes 24608 | tf_op jit(solution)/shard_map/ppermute | solution.py:24
  262.3 37.5 %psum.95 = f32[3,8,3,3,3]{1,4,3,2,0:T(4,128)} all-reduce(f32[3,8,3,3,3]{1,4,3,2,0:T(4,128)S(1)} %copy.170), channel_id=1, replica_groups=mesh['crops'=2,'xy'=4,'gz'=2,'lab'=2] {'xy','gz'}, use_global_device_ids=true, to_apply=%region_20.21 | all-reduce | flops 648 | bytes 5184 | tf_op jit(solution)/shard_map/psum | solution.py:172
  (370 shorter events, 82.0 us)
Async XLA Ops:
  7.2 55.5 %all-reduce.13.cloned.1.call-start = ((), (), s32[]{:S(2)}) async-start(), calls=%async_computation | async-start | bytes 262144 | tf_op jit(solution)/shard_map/psum | solution.py:70
  8.4 14.6 %collective-permute-start.1 = (bf16[8,1,32,128]{3,0,2,1:T(8,128)(2,1)S(1)}, bf16[8,1,32,128]{3,0,2,1:T(8,128)(2,1)S(1)}, u32[]{:S(2)}, u32[]{:S(2)}) collective-permute-start(bf16[8,1,32,128]{3,0,2,1:T(8,128)(2,1)S(1)} %get-tuple-element.39), channel_id=1, source_target_pairs={{4,0},{8,4},{12,8},{5,1},{9,5},{13,9},{6,2},{10,6},{14,10},{7,3},{... | collective-permute-start | bytes 196616 | tf_op jit(solution)/shard_map/ppermute | solution.py:24
  9.7 13.1 %collective-permute-start = (bf16[8,1,32,128]{3,0,2,1:T(8,128)(2,1)S(1)}, bf16[8,1,32,128]{3,0,2,1:T(8,128)(2,1)S(1)}, u32[]{:S(2)}, u32[]{:S(2)}) collective-permute-start(bf16[8,1,32,128]{3,0,2,1:T(8,128)(2,1)S(1)} %get-tuple-element.40), channel_id=1, source_target_pairs={{0,4},{4,8},{8,12},{1,5},{5,9},{9,13},{2,6},{6,10},{10,14},{3,7},{... | collective-permute-start | bytes 196616 | tf_op jit(solution)/shard_map/ppermute | solution.py:22
  16.2 11.6 %collective-permute-start.4 = (bf16[4,1,32,128]{3,2,1,0:T(8,128)(2,1)S(1)}, bf16[4,1,32,128]{3,2,1,0:T(8,128)(2,1)S(1)}, u32[]{:S(2)}, u32[]{:S(2)}) collective-permute-start(bf16[4,1,32,128]{3,2,1,0:T(8,128)(2,1)S(1)} %get-tuple-element.57), channel_id=1, source_target_pairs={{0,4},{4,8},{8,12},{1,5},{5,9},{9,13},{2,6},{6,10},{10,14},{3,7},{... | collective-permute-start | bytes 98312 | tf_op jit(solution)/shard_map/ppermute | solution.py:22
  20.3 7.5 %collective-permute-start.5 = (bf16[4,1,32,128]{3,2,1,0:T(8,128)(2,1)S(1)}, bf16[4,1,32,128]{3,2,1,0:T(8,128)(2,1)S(1)}, u32[]{:S(2)}, u32[]{:S(2)}) collective-permute-start(bf16[4,1,32,128]{3,2,1,0:T(8,128)(2,1)S(1)} %get-tuple-element.58), channel_id=1, source_target_pairs={{4,0},{8,4},{12,8},{5,1},{9,5},{13,9},{6,2},{10,6},{14,10},{7,3},{... | collective-permute-start | bytes 98312 | tf_op jit(solution)/shard_map/ppermute | solution.py:24
  23.1 10.6 %collective-permute-start.2 = (bf16[8,6,1,128]{3,0,2,1:T(8,128)(2,1)S(1)}, bf16[8,6,1,128]{3,0,2,1:T(8,128)(2,1)S(1)}, u32[]{:S(2)}, u32[]{:S(2)}) collective-permute-start(bf16[8,6,1,128]{3,0,2,1:T(8,128)(2,1)S(1)} %get-tuple-element.28), channel_id=1, source_target_pairs={{0,2},{1,3},{4,6},{5,7},{8,10},{9,11},{12,14},{13,15},{16,18},{17,... | collective-permute-start | bytes 36872 | tf_op jit(solution)/shard_map/ppermute | solution.py:22
  26.5 7.2 %collective-permute-start.3 = (bf16[8,6,1,128]{3,0,2,1:T(8,128)(2,1)S(1)}, bf16[8,6,1,128]{3,0,2,1:T(8,128)(2,1)S(1)}, u32[]{:S(2)}, u32[]{:S(2)}) collective-permute-start(bf16[8,6,1,128]{3,0,2,1:T(8,128)(2,1)S(1)} %get-tuple-element.29), channel_id=1, source_target_pairs={{2,0},{3,1},{6,4},{7,5},{10,8},{11,9},{14,12},{15,13},{18,16},{19,... | collective-permute-start | bytes 36872 | tf_op jit(solution)/shard_map/ppermute | solution.py:24
  27.8 14.4 %collective-permute-start.6 = (bf16[4,6,1,128]{3,2,1,0:T(2,128)(2,1)S(1)}, bf16[4,6,1,128]{3,2,1,0:T(2,128)(2,1)S(1)}, u32[]{:S(2)}, u32[]{:S(2)}) collective-permute-start(bf16[4,6,1,128]{3,2,1,0:T(2,128)(2,1)S(1)} %get-tuple-element.49), channel_id=1, source_target_pairs={{0,2},{1,3},{4,6},{5,7},{8,10},{9,11},{12,14},{13,15},{16,18},{17,... | collective-permute-start | bytes 18440 | tf_op jit(solution)/shard_map/ppermute | solution.py:22
  32.4 9.8 %collective-permute-start.7 = (bf16[4,6,1,128]{3,2,1,0:T(2,128)(2,1)S(1)}, bf16[4,6,1,128]{3,2,1,0:T(2,128)(2,1)S(1)}, u32[]{:S(2)}, u32[]{:S(2)}) collective-permute-start(bf16[4,6,1,128]{3,2,1,0:T(2,128)(2,1)S(1)} %get-tuple-element.50), channel_id=1, source_target_pairs={{2,0},{3,1},{6,4},{7,5},{10,8},{11,9},{14,12},{15,13},{18,16},{19,... | collective-permute-start | bytes 18440 | tf_op jit(solution)/shard_map/ppermute | solution.py:24
  42.2 196.1 %all-reduce.15.cloned.1.call-start = ((), (), s32[]{:S(2)}) async-start(), calls=%async_computation.1 | async-start | bytes 524288 | tf_op jit(solution)/shard_map/psum | solution.py:144
  64.4 7.6 %collective-permute-start.9 = (f32[4,1,128]{2,0,1:T(4,128)S(1)}, f32[4,1,128]{2,0,1:T(4,128)S(1)}, u32[]{:S(2)}, u32[]{:S(2)}) collective-permute-start(f32[4,1,128]{2,0,1:T(4,128)S(1)} %bitcast.468), channel_id=1, source_target_pairs={{0,2},{1,3},{4,6},{5,7},{8,10},{9,11},{12,14},{13,15},{16,18},{17,... | collective-permute-start | bytes 6152 | tf_op jit(solution)/shard_map/ppermute | solution.py:34
  68.4 4.8 %collective-permute-start.8 = (f32[1,32,128]{2,1,0:T(8,128)S(1)}, f32[1,32,128]{2,1,0:T(8,128)S(1)}, u32[]{:S(2)}, u32[]{:S(2)}) collective-permute-start(f32[1,32,128]{2,1,0:T(8,128)S(1)} %bitcast.466), channel_id=1, source_target_pairs={{0,4},{4,8},{8,12},{1,5},{5,9},{9,13},{2,6},{6,10},{10,14},{3,7},{... | collective-permute-start | bytes 49160 | tf_op jit(solution)/shard_map/ppermute | solution.py:34
  125.8 5.8 %collective-permute-start.11 = (bf16[4,1,32,128]{3,2,1,0:T(8,128)(2,1)S(1)}, bf16[4,1,32,128]{3,2,1,0:T(8,128)(2,1)S(1)}, u32[]{:S(2)}, u32[]{:S(2)}) collective-permute-start(bf16[4,1,32,128]{3,2,1,0:T(8,128)(2,1)S(1)} %get-tuple-element.56), channel_id=1, source_target_pairs={{4,0},{8,4},{12,8},{5,1},{9,5},{13,9},{6,2},{10,6},{14,10},{7,3},{... | collective-permute-start | bytes 98312 | tf_op jit(solution)/shard_map/ppermute | solution.py:24
  134.0 5.6 %collective-permute-start.13 = (bf16[4,6,1,128]{3,2,1,0:T(2,128)(2,1)S(1)}, bf16[4,6,1,128]{3,2,1,0:T(2,128)(2,1)S(1)}, u32[]{:S(2)}, u32[]{:S(2)}) collective-permute-start(bf16[4,6,1,128]{3,2,1,0:T(2,128)(2,1)S(1)} %get-tuple-element.48), channel_id=1, source_target_pairs={{2,0},{3,1},{6,4},{7,5},{10,8},{11,9},{14,12},{15,13},{18,16},{19,... | collective-permute-start | bytes 18440 | tf_op jit(solution)/shard_map/ppermute | solution.py:24
  174.6 4.9 %collective-permute-start.14 = (bf16[4,1,32,128]{3,2,1,0:T(8,128)(2,1)S(1)}, bf16[4,1,32,128]{3,2,1,0:T(8,128)(2,1)S(1)}, u32[]{:S(2)}, u32[]{:S(2)}) collective-permute-start(bf16[4,1,32,128]{3,2,1,0:T(8,128)(2,1)S(1)} %get-tuple-element.53), channel_id=1, source_target_pairs={{0,4},{4,8},{8,12},{1,5},{5,9},{9,13},{2,6},{6,10},{10,14},{3,7},{... | collective-permute-start | bytes 98312 | tf_op jit(solution)/shard_map/ppermute | solution.py:22
  178.0 5.8 %collective-permute-start.15 = (bf16[4,1,32,128]{3,2,1,0:T(8,128)(2,1)S(1)}, bf16[4,1,32,128]{3,2,1,0:T(8,128)(2,1)S(1)}, u32[]{:S(2)}, u32[]{:S(2)}) collective-permute-start(bf16[4,1,32,128]{3,2,1,0:T(8,128)(2,1)S(1)} %get-tuple-element.54), channel_id=1, source_target_pairs={{4,0},{8,4},{12,8},{5,1},{9,5},{13,9},{6,2},{10,6},{14,10},{7,3},{... | collective-permute-start | bytes 98312 | tf_op jit(solution)/shard_map/ppermute | solution.py:24
  183.8 5.4 %collective-permute-start.16 = (bf16[4,6,1,128]{3,2,1,0:T(2,128)(2,1)S(1)}, bf16[4,6,1,128]{3,2,1,0:T(2,128)(2,1)S(1)}, u32[]{:S(2)}, u32[]{:S(2)}) collective-permute-start(bf16[4,6,1,128]{3,2,1,0:T(2,128)(2,1)S(1)} %get-tuple-element.45), channel_id=1, source_target_pairs={{0,2},{1,3},{4,6},{5,7},{8,10},{9,11},{12,14},{13,15},{16,18},{17,... | collective-permute-start | bytes 18440 | tf_op jit(solution)/shard_map/ppermute | solution.py:22
  187.7 5.6 %collective-permute-start.17 = (bf16[4,6,1,128]{3,2,1,0:T(2,128)(2,1)S(1)}, bf16[4,6,1,128]{3,2,1,0:T(2,128)(2,1)S(1)}, u32[]{:S(2)}, u32[]{:S(2)}) collective-permute-start(bf16[4,6,1,128]{3,2,1,0:T(2,128)(2,1)S(1)} %get-tuple-element.46), channel_id=1, source_target_pairs={{2,0},{3,1},{6,4},{7,5},{10,8},{11,9},{14,12},{15,13},{18,16},{19,... | collective-permute-start | bytes 18440 | tf_op jit(solution)/shard_map/ppermute | solution.py:24
  211.5 7.7 %collective-permute-start.19 = (f32[8,4,1,128]{3,2,1,0:T(1,128)S(1)}, f32[8,4,1,128]{3,2,1,0:T(1,128)S(1)}, u32[]{:S(2)}, u32[]{:S(2)}) collective-permute-start(f32[8,4,1,128]{3,2,1,0:T(1,128)S(1)} %fusion.176), channel_id=1, source_target_pairs={{2,0},{3,1},{6,4},{7,5},{10,8},{11,9},{14,12},{15,13},{18,16},{19,... | collective-permute-start | bytes 49160 | tf_op jit(solution)/shard_map/ppermute | solution.py:34
  212.9 6.2 %collective-permute-start.18 = (bf16[8,1,32,128]{3,2,1,0:T(8,128)(2,1)S(1)}, bf16[8,1,32,128]{3,2,1,0:T(8,128)(2,1)S(1)}, u32[]{:S(2)}, u32[]{:S(2)}) collective-permute-start(bf16[8,1,32,128]{3,2,1,0:T(8,128)(2,1)S(1)} %fusion.141), channel_id=1, source_target_pairs={{4,0},{8,4},{12,8},{5,1},{9,5},{13,9},{6,2},{10,6},{14,10},{7,3},{... | collective-permute-start | bytes 196616 | tf_op jit(solution)/shard_map/ppermute | solution.py:34
  247.8 5.3 %collective-permute-start.20 = (bf16[3,1,32,128]{3,0,2,1:T(4,128)(2,1)S(1)}, bf16[3,1,32,128]{3,0,2,1:T(4,128)(2,1)S(1)}, u32[]{:S(2)}, u32[]{:S(2)}) collective-permute-start(bf16[3,1,32,128]{3,0,2,1:T(4,128)(2,1)S(1)} %get-tuple-element.51), channel_id=1, source_target_pairs={{0,4},{4,8},{8,12},{1,5},{5,9},{9,13},{2,6},{6,10},{10,14},{3,7},{... | collective-permute-start | bytes 73736 | tf_op jit(solution)/shard_map/ppermute | solution.py:22
  251.4 5.8 %collective-permute-start.21 = (bf16[3,1,32,128]{3,0,2,1:T(4,128)(2,1)S(1)}, bf16[3,1,32,128]{3,0,2,1:T(4,128)(2,1)S(1)}, u32[]{:S(2)}, u32[]{:S(2)}) collective-permute-start(bf16[3,1,32,128]{3,0,2,1:T(4,128)(2,1)S(1)} %get-tuple-element.52), channel_id=1, source_target_pairs={{4,0},{8,4},{12,8},{5,1},{9,5},{13,9},{6,2},{10,6},{14,10},{7,3},{... | collective-permute-start | bytes 73736 | tf_op jit(solution)/shard_map/ppermute | solution.py:24
  257.3 42.6 %collective-permute-start.22 = (bf16[3,6,1,128]{3,0,2,1:T(4,128)(2,1)S(1)}, bf16[3,6,1,128]{3,0,2,1:T(4,128)(2,1)S(1)}, u32[]{:S(2)}, u32[]{:S(2)}) collective-permute-start(bf16[3,6,1,128]{3,0,2,1:T(4,128)(2,1)S(1)} %get-tuple-element.43), channel_id=1, source_target_pairs={{0,2},{1,3},{4,6},{5,7},{8,10},{9,11},{12,14},{13,15},{16,18},{17,... | collective-permute-start | bytes 13832 | tf_op jit(solution)/shard_map/ppermute | solution.py:22
  260.6 39.2 %collective-permute-start.23 = (bf16[3,6,1,128]{3,0,2,1:T(4,128)(2,1)S(1)}, bf16[3,6,1,128]{3,0,2,1:T(4,128)(2,1)S(1)}, u32[]{:S(2)}, u32[]{:S(2)}) collective-permute-start(bf16[3,6,1,128]{3,0,2,1:T(4,128)(2,1)S(1)} %get-tuple-element.44), channel_id=1, source_target_pairs={{2,0},{3,1},{6,4},{7,5},{10,8},{11,9},{14,12},{15,13},{18,16},{19,... | collective-permute-start | bytes 13832 | tf_op jit(solution)/shard_map/ppermute | solution.py:24
  (90 other events, 796.8 us)
Sparse Core Ops, SparseCore 0:
  42.3 20.3 all-reduce.12
  220.7 17.5 all-reduce.14
